TPU v7x, 256 devices: a whole 4x4x8 slice. The times are simulated.
256 devices in a mesh: rows: 16 (over z_lo, y, core), tm: 16 (over x, z_hi).
Axes of the slice: x: 4, y: 4, z: 8 (z_hi: 4, z_lo: 2; z = z_hi * 2 + z_lo), core: 2. Of those that a mesh axis runs over, the one named last changes fastest.
Arguments:
- residual: float32 [64, 1024, 512], P('tm', 'rows'), may hold values from -45 to 45
- cycle_weight: float32 [64, 1024, 512], P('tm', 'rows'), may hold values from -0.75 to 0.75
- cycle_offsets: int32 [64, 2], replicated, may hold values from -6 to 6, as said below
Outputs:
- new_weight: float32 [64, 1024, 512], P('tm', 'rows')
- error: float32 [64, 1024, 512], P('tm', 'rows')
Inputs may be any that keep to these rules, and one draw needn't show every extreme that they name: `cycle_offsets`: each row is a distinct (row, column) offset; together the rows are the 64 pixels (dy, dx) with 17 <= dy*dy + dx*dx <= 36, in an order drawn from the seed.
All inputs are finite; a program needn't handle non-finite values.
Results may differ from a plain program's by a relative error of at most 0.0003.
Values sent between devices are 32-bit elements; how exact they have to be, the bound alone decides.
A program may use at most 64 MiB of HBM per device.

v0:
```python
import jax
import jax.numpy as jnp
import numpy as np
from jax import lax
from jax.sharding import PartitionSpec as P


def with_halo(cells, sides, width):
    for axis, dim in sides:
        count = lax.axis_size(axis)
        ends = count - 1
        head = lax.slice_in_dim(cells, 0, width, axis=dim)
        tail = lax.slice_in_dim(cells, cells.shape[dim] - width, cells.shape[dim], axis=dim)
        cells = jnp.concatenate(
            [
                lax.ppermute(tail, axis, [(i, (i + 1) % count) for i in range(ends)]),
                cells,
                lax.ppermute(head, axis, [((i + 1) % count, i) for i in range(ends)]),
            ],
            axis=dim,
        )
    return cells


def cycle_points():
    points = []
    for row_off in range(-6, 7):
        for col_off in range(-6, 7):
            radius = row_off * row_off + col_off * col_off
            if radius >= 17 and radius <= 36:
                points.append((row_off, col_off))
    return points


def matching(cycle_offsets, points):
    table_rows = jnp.asarray(np.array([p[0] for p in points], dtype=np.int32))
    table_cols = jnp.asarray(np.array([p[1] for p in points], dtype=np.int32))
    same = (table_rows[:, None] == cycle_offsets[None, :, 0]) & (
        table_cols[:, None] == cycle_offsets[None, :, 1]
    )
    return same.astype(jnp.float32)


def reorder(selector, weights):
    return jnp.einsum("jk,kyx->jyx", selector, weights, precision=lax.Precision.HIGHEST)


def window_of(padded, point, height, width):
    return padded[:, 6 + point[0] : 6 + point[0] + height, 6 + point[1] : 6 + point[1] + width]


def cycle_passes(padded, centre, ordered_weight, points, height, width):
    background = jnp.zeros(centre.shape, jnp.float32)
    for index, point in enumerate(points):
        background = background + ordered_weight[index][None] * window_of(
            padded, point, height, width
        )
    error_part = centre - background
    grads = jnp.stack(
        [jnp.sum(error_part * window_of(padded, point, height, width), axis=0) for point in points]
    )
    squares = jnp.sum(padded * padded, axis=0)
    energy_sum = jnp.zeros((height, width), jnp.float32)
    for point in points:
        energy_sum = (
            energy_sum
            + squares[6 + point[0] : 6 + point[0] + height, 6 + point[1] : 6 + point[1] + width]
        )
    return (error_part, grads, energy_sum)


def on_device(residual, cycle_weight, cycle_offsets):
    frames_dev, rows_dev, cols = residual.shape
    cycle = cycle_offsets.shape[0]
    tm_count = lax.axis_size("tm")
    frames_all = frames_dev * tm_count
    points = cycle_points()
    selector = matching(cycle_offsets, points)
    extended = with_halo(residual, (("rows", 1),), 6)
    padded = jnp.pad(extended, ((0, 0), (0, 0), (6, 6)))
    columns = selector
    ordered_weight = reorder(columns, lax.all_gather(cycle_weight, "tm", axis=0, tiled=True))
    error, ordered_grad, local_energy = cycle_passes(
        padded, residual, ordered_weight, points, rows_dev, cols
    )
    columns = selector
    gradient = lax.psum_scatter(
        jnp.einsum("jk,jyx->kyx", columns, ordered_grad, precision=lax.Precision.HIGHEST),
        "tm",
        scatter_dimension=0,
        tiled=True,
    )
    energy = lax.psum(local_energy, "tm") / (cycle * frames_all) + 1e-06
    new_weight = cycle_weight + gradient / (frames_all * energy)[None]
    return (new_weight, error)


def solution(mesh):
    in_specs = (P("tm", "rows", None), P("tm", "rows", None), P())
    out_specs = (P("tm", "rows", None), P("tm", "rows", None))
    return jax.shard_map(
        on_device, mesh=mesh, in_specs=in_specs, out_specs=out_specs, check_vma=False
    )
```

profile of v0, /device:TPU:4, one launch (start us, length us, event | category | flops | bytes accessed | tf_op | source)
XLA Modules:
  0.0 429.7 jit_solution(9261241765014633690)
XLA Ops:
  8.0 0.9 fusion.19
  8.9 1.7 collective-permute-start
  10.6 1.3 collective-permute-start.1
  11.9 0.8 slice_bitcast_fusion.1
  12.7 1.1 constant_dynamic-update-slice_fusion.1
  13.8 1.4 collective-permute-done.1
  15.1 1.4 multiply_reduce_fusion
  16.5 2.8 slice_add_fusion
  19.9 97.1 %all-gather.2.cloned.1.call-done = f32[64,64,512]{2,1,0:T(8,128)} async-done(((f32[4,64,512]{2,1,0:T(8,128)}), f32[64,64,512]{2,1,0:T(8,128)}) %all-gather.2.cloned.1.call-update) | async-done | bytes 8388624 | tf_op jit(solution)/shard_map/all_gather | solution.py:82
  117.0 13.4 %fusion = f32[64,64,512]{2,0,1:T(8,128)S(1)} fusion(f32[64,64,512]{2,1,0:T(8,128)} %all-gather.2.cloned.1.call-done, s32[64]{0:T(128)S(1)} %copy-done.4, s32[64]{0:T(128)S(1)} %copy-done.3, s32[64]{0:T(128)S(1)} %get-tuple-element.146, s32[64]{0:T(128)S(1)} %get-tuple-element.145), kind=kOutput, calls=%fused_computation | convolution fusion | flops 1610625024 | bytes 16778240 | tf_op jit(solution)/shard_map/jk,kyx->jyx/dot_general | solution.py:45
  130.5 2.0 fusion.17
  132.4 2.3 fusion.15
  134.7 2.4 fusion.16
  138.8 9.4 %multiply_reduce_fusion.2 = (f32[64,512]{1,0:T(8,128)S(1)}, f32[64,512]{1,0:T(8,128)S(1)}, f32[64,512]{1,0:T(8,128)S(1)}, f32[64,512]{1,0:T(8,128)S(1)}, f32[64,...) fusion(f32[4,76,524]{2,1,0:T(8,128)S(1)} %get-tuple-element.142, ...), kind=kLoop, calls=%fused_computation.14 | loop fusion | flops 21168128 | bytes 44351488 | tf_op jit(solution)/shard_map/reduce_sum | solution.py:60
  148.3 2.5 multiply_reduce_fusion.39
  150.8 2.4 multiply_reduce_fusion.21
  154.3 0.7 stack.214
  155.0 0.7 stack.215
  156.5 0.7 stack.217
  157.9 0.7 stack.219
  158.7 0.7 stack.220
  159.4 0.7 stack.221
  161.6 0.7 stack.224
  163.1 0.7 stack.226
  163.9 0.7 stack.227
  164.6 0.7 stack.228
  166.1 0.7 stack.230
  166.8 0.7 stack.231
  167.6 0.7 stack.232
  168.3 0.7 stack.233
  169.1 0.7 stack.234
  171.3 0.7 stack.237
  172.0 0.7 stack.238
  172.7 0.9 multiply_reduce_fusion.1
  178.7 0.8 stack.248
  179.4 0.7 stack.249
  181.7 0.7 stack.252
  182.4 0.7 stack.253
  183.1 1.0 stack.255
  184.1 0.7 stack.256
  184.8 0.7 stack.257
  185.6 28.8 %stack.259 = f32[64,64,512]{2,0,1:T(8,128)} concatenate(f32[1,64,512]{2,0,1:T(1,128)S(1)} %stack.195, f32[1,64,512]{2,0,1:T(1,128)S(1)} %stack.196, f32[1,64,512]{2,0,1:T(1,128)S(1)} %stack.197, f32[1,64,512]{2,0,1:T(1,128)S(1)} %stack.198, f32[1,64,512]{2,0,1:T(1,128)S(1)} %stack.199, f32[1,64,512]{2,0,1:T(1,128)S(1)} %stack.200, f32[1,64,512]{2,0,1:T(1,128)S(1)} %stack.201, ...), dimensions={0} | concatenate | bytes 16777216 | tf_op jit(solution)/shard_map/stack | solution.py:59
  214.3 8.2 %fusion.5 = f32[64,64,512]{2,0,1:T(8,128)S(1)} fusion(f32[64,64,512]{2,0,1:T(8,128)} %stack.259, s32[64]{0:T(128)S(1)} %copy-done.4, s32[64]{0:T(128)S(1)} %copy-done.3, s32[64]{0:T(128)S(1)} %get-tuple-element.146, s32[64]{0:T(128)S(1)} %get-tuple-element.145), kind=kOutput, calls=%fused_computation.207 | convolution fusion | flops 1610625024 | bytes 16778240 | tf_op jit(solution)/shard_map/jk,jyx->kyx/dot_general | solution.py:88
  222.5 8.1 %copy.13 = f32[64,64,512]{2,1,0:T(8,128)} copy(f32[64,64,512]{2,0,1:T(8,128)S(1)} %fusion.5) | data formatting | bytes 16777216 | tf_op jit(solution)/shard_map/jk,jyx->kyx/dot_general | solution.py:88
  230.6 62.9 %all-reduce.3.cloned.1.call-done = f32[64,512]{1,0:T(8,128)} async-done(((f32[64,512]{1,0:T(8,128)}), f32[64,512]{1,0:T(8,128)}) %all-reduce.3.cloned.1.call-update) | async-done | bytes 131088 | tf_op jit(solution)/shard_map/psum | solution.py:93
  293.5 0.9 add_multiply_fusion
  294.4 126.6 %reduce-scatter.2.cloned.1.call-done = f32[4,64,512]{2,1,0:T(8,128)} async-done(((f32[64,64,512]{2,1,0:T(8,128)}), f32[4,64,512]{2,1,0:T(8,128)}) %reduce-scatter.2.cloned.1.call-update) | async-done | bytes 524304 | tf_op jit(solution)/shard_map/reduce_scatter | solution.py:87
  421.0 1.9 divide_add_fusion
  (91 shorter events, 16.0 us)
Async XLA Ops:
  7.2 109.9 %copy-start.3 = (s32[64]{0:T(128)S(1)}, s32[64]{0:T(128)}, u32[]{:S(2)}) copy-start(s32[64]{0:T(128)} %constant.15.clone) | copy-start | bytes 772
  7.2 109.9 %copy-start.4 = (s32[64]{0:T(128)S(1)}, s32[64]{0:T(128)}, u32[]{:S(2)}) copy-start(s32[64]{0:T(128)} %constant.16.clone) | copy-start | bytes 772
  7.2 109.8 %all-gather.2.cloned.1.call-start = ((), (), s32[]{:S(2)}) async-start(), calls=%async_computation.1 | async-start | bytes 8912896 | tf_op jit(solution)/shard_map/all_gather | solution.py:82
  7.9 285.6 %all-reduce.3.cloned.1.call-start = ((), (), s32[]{:S(2)}) async-start(), calls=%async_computation.3 | async-start | bytes 262144 | tf_op jit(solution)/shard_map/psum | solution.py:93
  8.9 4.9 %collective-permute-start = (f32[4,6,512]{2,1,0:T(8,128)S(1)}, f32[4,6,512]{2,1,0:T(8,128)S(1)}, u32[]{:S(2)}, u32[]{:S(2)}) collective-permute-start(f32[4,6,512]{2,1,0:T(8,128)S(1)} %get-tuple-element.143), channel_id=1, source_target_pairs={{0,16},{16,32},{32,48},{48,64},{64,80},{80,96},{96,112},{112,128},... | collective-permute-start | bytes 147464 | tf_op jit(solution)/shard_map/ppermute | solution.py:16
  10.6 4.5 %collective-permute-start.1 = (f32[4,6,512]{2,1,0:T(8,128)S(1)}, f32[4,6,512]{2,1,0:T(8,128)S(1)}, u32[]{:S(2)}, u32[]{:S(2)}) collective-permute-start(f32[4,6,512]{2,1,0:T(8,128)S(1)} %get-tuple-element.144), channel_id=1, source_target_pairs={{16,0},{32,16},{48,32},{64,48},{80,64},{96,80},{112,96},{128,112},... | collective-permute-start | bytes 147464 | tf_op jit(solution)/shard_map/ppermute | solution.py:18
  19.4 401.6 %reduce-scatter.2.cloned.1.call-start = ((), (), s32[]{:S(2)}) async-start(), calls=%async_computation.2 | async-start | bytes 8912896 | tf_op jit(solution)/shard_map/reduce_scatter | solution.py:87
  137.8 1.0 copy-start
  148.3 24.5 %copy-start.1 = (f32[4,64,512]{2,1,0:T(8,128)}, f32[4,64,512]{2,1,0:T(8,128)S(1)}, u32[]{:S(2)}) copy-start(f32[4,64,512]{2,1,0:T(8,128)S(1)} %get-tuple-element.76) | copy-start | bytes 1572868
  230.6 190.4 %copy-start.2 = (f32[4,64,512]{2,1,0:T(8,128)S(1)}, f32[4,64,512]{2,1,0:T(8,128)}, u32[]{:S(2)}) copy-start(f32[4,64,512]{2,1,0:T(8,128)} %param.6) | copy-start | bytes 1572868
Sparse Core Ops, SparseCore 0:
  10.4 106.5 all-gather.1
  119.6 173.7 all-reduce.2
  297.2 123.7 reduce-scatter.1
where the time goes:
time: 434 us; the launch traced here: 430 us
  waiting for transfers between devices  289 us (67%)
  local copies, waits for them, and re-layouts  79 us (18%)
  other arithmetic  22.3 us (5%)
  matrix products  21.6 us (5%)
  between operations  14.6 us (3%)
    reduce_scatter x1, waiting for transfers between devices, on_device(): lax.psum_scatter(jnp.einsum('jk,jyx->kyx', columns, ordered_grad, precisi...  127 us
    all_gather x1, waiting for transfers between devices, on_device(): lax.all_gather(cycle_weight, 'tm', axis=0, tiled=True)  97.1 us
    psum x1, waiting for transfers between devices, on_device(): energy = lax.psum(local_energy, 'tm') / (cycle * frames_all) + 1e-06  62.9 us
    another operation x65, local copies, waits for them, and re-layouts, cycle_passes(): jnp.stack([jnp.sum(error_part * window_of(padded, point, height, width),...  60.1 us
    reduce_sum x4, other arithmetic, cycle_passes(): jnp.sum(error_part * window_of(padded, point, height, width), axis=0)  15.2 us
    dot_general x1, matrix products, reorder(): jnp.einsum('jk,kyx->jyx', selector, weights, precision=lax.Precision.HIGH...  13.4 us
  transfers between devices with their start and end apart: 5, of which 4 were waited for; matrix products, arithmetic and copies ran while one was open for 28% of the time, Pallas kernels for 0%

commit v1 on v0

--- a/solution.py
+++ b/solution.py
@@ -70,6 +70,11 @@
 
 
 def on_device(residual, cycle_weight, cycle_offsets):
+
+    def groups_start(page):
+        outcome_arr = lax.all_gather(page, axis_name="tm")
+        return jnp.sum(outcome_arr, axis=0)
+
     frames_dev, rows_dev, cols = residual.shape
     cycle = cycle_offsets.shape[0]
     tm_count = lax.axis_size("tm")
@@ -90,7 +95,7 @@
         scatter_dimension=0,
         tiled=True,
     )
-    energy = lax.psum(local_energy, "tm") / (cycle * frames_all) + 1e-06
+    energy = groups_start(local_energy) / (cycle * frames_all) + 1e-06
     new_weight = cycle_weight + gradient / (frames_all * energy)[None]
     return (new_weight, error)
 

time: 434 us -> 377 us (0.87)
  waiting for transfers between devices: 289 us -> 231 us
    psum x1 -> x0, waiting for transfers between devices: 62.9 us -> none  [on_device(): energy = lax.psum(local_energy, 'tm') / (cycle * frames_all) + 1e-06]
    reduce_scatter x1, waiting for transfers between devices: 127 us -> 132 us  [on_device(): lax.psum_scatter(jnp.einsum('jk,jyx->kyx', columns, ordered_grad, precisi...]
  transfers between devices with their start and end apart: 5 -> 5, of which waited for: 4 -> 3; matrix products, arithmetic and copies ran while one was open for 28% -> 32% of each run, Pallas kernels for 0% -> 0%
where the time goes in v1:
time: 377 us; the launch traced here: 372 us
  waiting for transfers between devices  231 us (61%)
  local copies, waits for them, and re-layouts  78.4 us (21%)
  other arithmetic  23.2 us (6%)
  matrix products  21.6 us (6%)
  between operations  14.6 us (4%)
    reduce_scatter x1, waiting for transfers between devices, on_device(): lax.psum_scatter(jnp.einsum('jk,jyx->kyx', columns, ordered_grad, precisi...  132 us
    all_gather x1, waiting for transfers between devices, on_device(): lax.all_gather(cycle_weight, 'tm', axis=0, tiled=True)  97.1 us
    another operation x65, local copies, waits for them, and re-layouts, cycle_passes(): jnp.stack([jnp.sum(error_part * window_of(padded, point, height, width),...  59.4 us
    reduce_sum x4, other arithmetic, cycle_passes(): jnp.sum(error_part * window_of(padded, point, height, width), axis=0)  15.2 us
    dot_general x1, matrix products, reorder(): jnp.einsum('jk,kyx->jyx', selector, weights, precision=lax.Precision.HIGH...  13.4 us
    dot_general x1, matrix products, on_device(): jnp.einsum('jk,jyx->kyx', columns, ordered_grad, precision=lax.Precision....  8.15 us
    dot_general x1, local copies, waits for them, and re-layouts, on_device(): jnp.einsum('jk,jyx->kyx', columns, ordered_grad, precision=lax.Precision....  8.08 us
  transfers between devices with their start and end apart: 5, of which 3 were waited for; matrix products, arithmetic and copies ran while one was open for 32% of the time, Pallas kernels for 0%

profile of v1, /device:TPU:4, one launch (start us, length us, event | category | flops | bytes accessed | tf_op | source)
XLA Modules:
  0.0 372.5 jit_solution(12245926401332277306)
XLA Ops:
  8.0 0.9 fusion.19
  8.9 1.7 collective-permute-start
  10.6 1.3 collective-permute-start.1
  11.9 0.8 slice_bitcast_fusion.1
  12.7 1.1 constant_dynamic-update-slice_fusion.1
  13.8 1.4 collective-permute-done.1
  15.1 1.4 multiply_reduce_fusion
  16.5 2.9 slice_add_fusion
  19.9 97.1 %all-gather.4.cloned.1.call-done = f32[64,64,512]{2,1,0:T(8,128)} async-done(((f32[4,64,512]{2,1,0:T(8,128)}), f32[64,64,512]{2,1,0:T(8,128)}) %all-gather.4.cloned.1.call-update) | async-done | bytes 8388624 | tf_op jit(solution)/shard_map/all_gather | solution.py:87
  117.0 13.4 %fusion = f32[64,64,512]{2,0,1:T(8,128)S(1)} fusion(f32[64,64,512]{2,1,0:T(8,128)} %all-gather.4.cloned.1.call-done, s32[64]{0:T(128)S(1)} %copy-done.4, s32[64]{0:T(128)S(1)} %copy-done.3, s32[64]{0:T(128)S(1)} %get-tuple-element.146, s32[64]{0:T(128)S(1)} %get-tuple-element.145), kind=kOutput, calls=%fused_computation | convolution fusion | flops 1610625024 | bytes 16778240 | tf_op jit(solution)/shard_map/jk,kyx->jyx/dot_general | solution.py:45
  130.5 1.9 fusion.17
  132.4 2.3 fusion.15
  134.7 2.5 fusion.16
  138.9 9.4 %multiply_reduce_fusion.2 = (f32[64,512]{1,0:T(8,128)S(1)}, f32[64,512]{1,0:T(8,128)S(1)}, f32[64,512]{1,0:T(8,128)S(1)}, f32[64,512]{1,0:T(8,128)S(1)}, f32[64,...) fusion(f32[4,76,524]{2,1,0:T(8,128)S(1)} %get-tuple-element.142, ...), kind=kLoop, calls=%fused_computation.14 | loop fusion | flops 21168128 | bytes 44351488 | tf_op jit(solution)/shard_map/reduce_sum | solution.py:60
  148.3 2.5 multiply_reduce_fusion.39
  152.3 0.7 stack.218
  153.8 0.7 stack.220
  154.6 2.4 multiply_reduce_fusion.21
  156.9 0.7 stack.221
  157.7 0.7 stack.222
  158.4 0.7 stack.223
  160.6 0.7 stack.226
  161.4 0.7 stack.227
  165.8 0.8 stack.233
  166.5 0.7 stack.234
  168.7 0.7 stack.237
  169.5 0.7 stack.238
  170.2 0.9 multiply_reduce_fusion.1
  172.2 0.7 stack.240
  172.9 0.7 stack.241
  173.7 0.7 stack.242
  174.4 0.7 stack.243
  175.2 0.7 stack.244
  176.6 0.7 stack.246
  177.4 0.7 stack.247
  178.1 0.7 stack.248
  179.6 0.7 stack.250
  181.1 0.7 stack.252
  181.8 0.7 stack.253
  182.5 1.0 stack.255
  183.5 0.7 stack.256
  184.2 0.7 stack.257
  185.0 28.7 %stack.259 = f32[64,64,512]{2,0,1:T(8,128)} concatenate(f32[1,64,512]{2,0,1:T(1,128)S(1)} %stack.195, f32[1,64,512]{2,0,1:T(1,128)S(1)} %stack.196, f32[1,64,512]{2,0,1:T(1,128)S(1)} %stack.197, f32[1,64,512]{2,0,1:T(1,128)S(1)} %stack.198, f32[1,64,512]{2,0,1:T(1,128)S(1)} %stack.199, f32[1,64,512]{2,0,1:T(1,128)S(1)} %stack.200, f32[1,64,512]{2,0,1:T(1,128)S(1)} %stack.201, ...), dimensions={0} | concatenate | bytes 16777216 | tf_op jit(solution)/shard_map/stack | solution.py:59
  213.7 8.2 %fusion.5 = f32[64,64,512]{2,0,1:T(8,128)S(1)} fusion(f32[64,64,512]{2,0,1:T(8,128)} %stack.259, s32[64]{0:T(128)S(1)} %copy-done.4, s32[64]{0:T(128)S(1)} %copy-done.3, s32[64]{0:T(128)S(1)} %get-tuple-element.146, s32[64]{0:T(128)S(1)} %get-tuple-element.145), kind=kOutput, calls=%fused_computation.207 | convolution fusion | flops 1610625024 | bytes 16778240 | tf_op jit(solution)/shard_map/jk,jyx->kyx/dot_general | solution.py:93
  221.9 8.1 %copy.16 = f32[64,64,512]{2,1,0:T(8,128)} copy(f32[64,64,512]{2,0,1:T(8,128)S(1)} %fusion.5) | data formatting | bytes 16777216 | tf_op jit(solution)/shard_map/jk,jyx->kyx/dot_general | solution.py:93
  230.0 1.8 reduce_sum.659
  231.9 131.9 %reduce-scatter.2.cloned.1.call-done = f32[4,64,512]{2,1,0:T(8,128)} async-done(((f32[64,64,512]{2,1,0:T(8,128)}), f32[4,64,512]{2,1,0:T(8,128)}) %reduce-scatter.2.cloned.1.call-update) | async-done | bytes 524304 | tf_op jit(solution)/shard_map/reduce_scatter | solution.py:92
  363.8 1.9 divide_add_fusion
  (92 shorter events, 14.7 us)
Async XLA Ops:
  7.2 109.9 %copy-start.3 = (s32[64]{0:T(128)S(1)}, s32[64]{0:T(128)}, u32[]{:S(2)}) copy-start(s32[64]{0:T(128)} %constant.15.clone) | copy-start | bytes 772
  7.2 109.9 %copy-start.4 = (s32[64]{0:T(128)S(1)}, s32[64]{0:T(128)}, u32[]{:S(2)}) copy-start(s32[64]{0:T(128)} %constant.16.clone) | copy-start | bytes 772
  7.2 109.8 %all-gather.4.cloned.1.call-start = ((), (), s32[]{:S(2)}) async-start(), calls=%async_computation.1 | async-start | bytes 8912896 | tf_op jit(solution)/shard_map/all_gather | solution.py:87
  7.9 222.1 %all-gather.6.cloned.1.call-start = ((), (), s32[]{:S(2)}) async-start(), calls=%async_computation.3 | async-start | bytes 2228224 | tf_op jit(solution)/shard_map/all_gather | solution.py:75
  8.9 4.9 %collective-permute-start = (f32[4,6,512]{2,1,0:T(8,128)S(1)}, f32[4,6,512]{2,1,0:T(8,128)S(1)}, u32[]{:S(2)}, u32[]{:S(2)}) collective-permute-start(f32[4,6,512]{2,1,0:T(8,128)S(1)} %get-tuple-element.143), channel_id=1, source_target_pairs={{0,16},{16,32},{32,48},{48,64},{64,80},{80,96},{96,112},{112,128},... | collective-permute-start | bytes 147464 | tf_op jit(solution)/shard_map/ppermute | solution.py:16
  10.6 4.5 %collective-permute-start.1 = (f32[4,6,512]{2,1,0:T(8,128)S(1)}, f32[4,6,512]{2,1,0:T(8,128)S(1)}, u32[]{:S(2)}, u32[]{:S(2)}) collective-permute-start(f32[4,6,512]{2,1,0:T(8,128)S(1)} %get-tuple-element.144), channel_id=1, source_target_pairs={{16,0},{32,16},{48,32},{64,48},{80,64},{96,80},{112,96},{128,112},... | collective-permute-start | bytes 147464 | tf_op jit(solution)/shard_map/ppermute | solution.py:18
  19.4 344.4 %reduce-scatter.2.cloned.1.call-start = ((), (), s32[]{:S(2)}) async-start(), calls=%async_computation.2 | async-start | bytes 8912896 | tf_op jit(solution)/shard_map/reduce_scatter | solution.py:92
  137.8 1.0 copy-start
  148.3 21.9 %copy-start.1 = (f32[4,64,512]{2,1,0:T(8,128)}, f32[4,64,512]{2,1,0:T(8,128)S(1)}, u32[]{:S(2)}) copy-start(f32[4,64,512]{2,1,0:T(8,128)S(1)} %get-tuple-element.76) | copy-start | bytes 1572868
  230.0 133.8 %copy-start.2 = (f32[4,64,512]{2,1,0:T(8,128)S(1)}, f32[4,64,512]{2,1,0:T(8,128)}, u32[]{:S(2)}) copy-start(f32[4,64,512]{2,1,0:T(8,128)} %param.6) | copy-start | bytes 1572868
Sparse Core Ops, SparseCore 0:
  10.4 106.5 all-gather.3
  119.5 70.7 all-gather.5
  230.1 133.6 reduce-scatter.1
